TPU v7x, 32 devices: a whole 2x2x4 slice. The times are simulated.
32 devices in a mesh: lon: 8 (over z, y), lat: 4 (over x, core).
Axes of the slice: x: 2, y: 2, z: 4, core: 2. Of those that a mesh axis runs over, the one named last changes fastest.
Arguments:
- ocean_state: float32 [4, 8, 64, 1024], P(None, None, 'lat', 'lon'), may hold values from -5 to 5
- thickness: float32 [8, 64, 1024], P(None, 'lat', 'lon'), may hold values from 0.5 to 2
- wet_mask: int32 [8, 64, 1024], P(None, 'lat', 'lon'), may hold values 0 or 1
- mode_counts: int32 [64], P('lat'), may hold values from 1 to 64, as said below
- row_flags: int32 [64], P('lat'), may hold values from 0 to 1, as said below
Outputs:
- ocean_next: float32 [4, 8, 64, 1024], P(None, None, 'lat', 'lon')
Inputs may be any that keep to these rules, and one draw needn't show every extreme that they name: `mode_counts`: mode counts lie in the range; row 0 keeps 64. `row_flags`: only rows among the first 16 or the last 16 are flagged; the first and the last row always are.
All inputs are finite; a program needn't handle non-finite values. No bound on the sum of `wet_mask` on one device may be relied on, other than what follows from the above.
Results may differ from a plain program's by a relative error of at most 0.0003.
Values sent between devices are 32-bit elements; how exact they have to be, the bound alone decides.
No kernel may reach another device: no remote copies, remote signals or barrier semaphores. Data moves between devices by JAX's collectives and lax.ppermute only.
A program may use at most 64 MiB of HBM per device.

v0:
```python
import math
import jax
import jax.numpy as jnp
from jax import lax
from jax.sharding import PartitionSpec as P

FBAND = 16
MAXM = 64
lat_edge = 1.3
diffusion = 0.05
vertical_mix = 0.5
time_step = 0.05


def with_halo(array, sides, width, wrap):
    for axis, dim in sides:
        peers, length = (lax.axis_size(axis), array.shape[dim])
        up = [(i, (i + 1) % peers) for i in range(peers if wrap else peers - 1)]
        down = [(j, i) for i, j in up]
        last = lax.slice_in_dim(array, length - width, length, axis=dim)
        leading = lax.slice_in_dim(array, 0, width, axis=dim)
        before = lax.ppermute(last, axis, up)
        after = lax.ppermute(leading, axis, down)
        array = jnp.concatenate([before, array, after], axis=dim)
    return array


def advance(padded, u_pad, v_pad, static, centre, faces):
    thick = static[0]
    wet = static[1]
    inv_c = 1.0 / centre
    east_u = 0.5 * (u_pad[:, :, :-1] + u_pad[:, :, 1:])
    east_h = 0.5 * (thick[:, :, :-1] + thick[:, :, 1:]) * wet[:, :, :-1] * wet[:, :, 1:]
    flux_e = east_h[None] * (
        east_u[None] * 0.5 * (padded[..., :-1] + padded[..., 1:])
        - diffusion * (padded[..., 1:] - padded[..., :-1]) * inv_c[:, None]
    )
    zonal = (flux_e[..., 1:] - flux_e[..., :-1])[:, :, 1:-1, :] * inv_c[1:-1, None]
    north_v = 0.5 * (v_pad[:, :-1, :] + v_pad[:, 1:, :])
    north_h = (
        0.5 * (thick[:, :-1, :] + thick[:, 1:, :]) * wet[:, :-1, :] * wet[:, 1:, :] * faces[:, None]
    )
    flux_n = north_h[None] * (
        north_v[None] * 0.5 * (padded[:, :, :-1] + padded[:, :, 1:])
        - diffusion * (padded[:, :, 1:] - padded[:, :, :-1])
    )
    merid = (flux_n[:, :, 1:] - flux_n[:, :, :-1])[..., 1:-1] * inv_c[1:-1, None]
    inner = padded[:, :, 1:-1, 1:-1]
    wet_in = wet[:, 1:-1, 1:-1]
    thick_in = jnp.where(wet_in > 0, thick[:, 1:-1, 1:-1], 1.0)
    coupling = wet_in[:-1] * wet_in[1:] * vertical_mix / (0.5 * (thick_in[:-1] + thick_in[1:]))
    vmix = coupling[None] * (inner[:, 1:] - inner[:, :-1])
    empty = jnp.zeros_like(vmix[:, :1])
    vert = jnp.concatenate([vmix, empty], axis=1) - jnp.concatenate([empty, vmix], axis=1)
    return inner + wet_in[None] * time_step * (vert - zonal - merid) / thick_in[None]


def mode_basis(index, length, modes):
    turns = jnp.arange(modes, dtype=jnp.int32)[None, :] * index[:, None] % length
    angle = turns.astype(jnp.float32) * (2.0 * math.pi / length)
    return jnp.concatenate([jnp.cos(angle), jnp.sin(angle)], axis=1)


def mode_weights(counts, modes, length):
    order = jnp.arange(modes).astype(jnp.float32)
    keep = (order[None, :] < counts[:, None]).astype(jnp.float32)
    scale = jnp.where(order == 0, 1.0, 2.0) / length
    weights = keep * scale[None, :]
    return jnp.concatenate([weights, weights], axis=1)


def extend(fields, width):
    wider = with_halo(fields, (("lon", 3),), width, True)
    return with_halo(wider, (("lat", 2),), width, False)


def shards(ocean_state, thickness, wet_mask, mode_counts, row_flags):
    wet = wet_mask.astype(jnp.float32)
    static = jnp.stack([thickness, wet])
    levels = ocean_state.shape[1]
    rows = ocean_state.shape[2]
    lanes = ocean_state.shape[3]
    nlat = rows * lax.axis_size("lat")
    nlon = lanes * lax.axis_size("lon")
    lat_pos = lax.axis_index("lat")
    lon_pos = lax.axis_index("lon")
    joined = extend(jnp.concatenate([ocean_state, static], axis=0), 1)
    fields = joined[:4]
    fixed = joined[4:]
    index = lat_pos * rows - 1 + jnp.arange(rows + 2 * 1, dtype=jnp.int32)
    place = index.astype(jnp.float32)
    centre = jnp.cos(lat_edge * (2.0 * (place + 0.5) / nlat - 1.0))
    faces = jnp.cos(lat_edge * (2.0 * (place[:-1] + 1.0) / nlat - 1.0))
    centre, faces = (centre, faces)
    state = advance(fields, fields[2], fields[3], fixed, centre, faces)
    fields = extend(state, 1)
    state = advance(fields, fields[2], fields[3], fixed, centre, faces)
    flags = row_flags.astype(jnp.float32)
    counts = mode_counts.astype(jnp.float32)
    total = 4 * levels * FBAND
    flat = state.reshape(total, lanes)
    row_counts = jnp.broadcast_to(counts[None, None, :], (4, levels, FBAND)).reshape(total)
    index = lon_pos * lanes + jnp.arange(lanes, dtype=jnp.int32)
    basis = mode_basis(index, nlon, MAXM)
    partial_sum = jnp.dot(
        flat, basis, precision=lax.Precision.HIGHEST, preferred_element_type=jnp.float32
    )
    totals = lax.psum(partial_sum, "lon")
    smooth = jnp.dot(
        totals * mode_weights(row_counts, MAXM, nlon),
        basis.T,
        precision=lax.Precision.HIGHEST,
        preferred_element_type=jnp.float32,
    )
    smooth = smooth.reshape(4, levels, FBAND, lanes)
    filtered = state + flags[None, None, :, None] * wet[None] * (smooth - state)
    return filtered


def solution(mesh):
    in_specs = (
        P(None, None, "lat", "lon"),
        P(None, "lat", "lon"),
        P(None, "lat", "lon"),
        P("lat"),
        P("lat"),
    )
    out_specs = P(None, None, "lat", "lon")
    return jax.shard_map(shards, mesh=mesh, in_specs=in_specs, out_specs=out_specs, check_vma=False)
```

profile of v0, /device:TPU:0, one launch (start us, length us, event | category | flops | bytes accessed | tf_op | source)
XLA Modules:
  0.0 145.7 jit_solution(13678122371583939406)
XLA Ops:
  6.5 0.8 convert_bitcast_fusion
  7.4 1.1 pad_maximum_fusion.13
  8.5 0.2 fusion.44
  8.7 6.1 %collective-permute-start.1 = (f32[6,8,16,1]{3,2,1,0:T(8,128)S(1)}, f32[6,8,16,1]{3,2,1,0:T(8,128)S(1)}, u32[]{:S(2)}, u32[]{:S(2)}) collective-permute-start(f32[6,8,16,1]{3,2,1,0:T(8,128)S(1)} %get-tuple-element.24), channel_id=1, source_target_pairs={{4,0},{8,4},{12,8},{16,12},{20,16},{24,20},{28,24},{0,28},{5,1},{9... | collective-permute-start | bytes 9224 | tf_op jit(solution)/shard_map/ppermute | solution.py:23
  14.8 0.3 fusion.35
  15.3 13.9 %collective-permute-done.1 = f32[6,8,16,1]{3,2,1,0:T(8,128)S(1)} collective-permute-done((f32[6,8,16,1]{3,2,1,0:T(8,128)S(1)}, f32[6,8,16,1]{3,2,1,0:T(8,128)S(1)}, u32[]{:S(2)}, u32[]{:S(2)}) %collective-permute-start.1) | collective-permute-done | bytes 3104 | tf_op jit(solution)/shard_map/ppermute | solution.py:23
  29.4 0.4 pad_maximum_fusion.15
  29.8 1.9 %collective-permute-start.2 = (f32[6,8,1,130]{3,2,1,0:T(1,128)S(1)}, f32[6,8,1,130]{3,2,1,0:T(1,128)S(1)}, u32[]{:S(2)}, u32[]{:S(2)}) collective-permute-start(f32[6,8,1,130]{3,2,1,0:T(1,128)S(1)} %get-tuple-element.10), channel_id=1, source_target_pairs={{0,1},{1,2},{2,3},{4,5},{5,6},{6,7},{8,9},{9,10},{10,11},{12,13},{... | collective-permute-start | bytes 74888 | tf_op jit(solution)/shard_map/ppermute | solution.py:22
  31.7 1.3 collective-permute-start.3
  33.1 2.9 %collective-permute-done.3 = f32[6,8,1,130]{3,2,1,0:T(1,128)S(1)} collective-permute-done((f32[6,8,1,130]{3,2,1,0:T(1,128)S(1)}, f32[6,8,1,130]{3,2,1,0:T(1,128)S(1)}, u32[]{:S(2)}, u32[]{:S(2)}) %collective-permute-start.3) | collective-permute-done | bytes 24992 | tf_op jit(solution)/shard_map/ppermute | solution.py:23
  36.0 0.5 pad_maximum_fusion
  36.8 0.6 subtract_multiply_fusion.2
  37.5 0.2 fusion.23
  37.8 0.3 subtract_multiply_fusion.3
  38.0 0.2 fusion.42
  38.4 0.3 fusion.11
  38.8 4.8 %collective-permute-start.5 = (f32[4,8,16,1]{3,2,1,0:T(8,128)S(1)}, f32[4,8,16,1]{3,2,1,0:T(8,128)S(1)}, u32[]{:S(2)}, u32[]{:S(2)}) collective-permute-start(f32[4,8,16,1]{3,2,1,0:T(8,128)S(1)} %get-tuple-element.26), channel_id=1, source_target_pairs={{4,0},{8,4},{12,8},{16,12},{20,16},{24,20},{28,24},{0,28},{5,1},{9... | collective-permute-start | bytes 6152 | tf_op jit(solution)/shard_map/ppermute | solution.py:23
  43.6 4.8 %collective-permute-done.5 = f32[4,8,16,1]{3,2,1,0:T(8,128)S(1)} collective-permute-done((f32[4,8,16,1]{3,2,1,0:T(8,128)S(1)}, f32[4,8,16,1]{3,2,1,0:T(8,128)S(1)}, u32[]{:S(2)}, u32[]{:S(2)}) %collective-permute-start.5) | collective-permute-done | bytes 2080 | tf_op jit(solution)/shard_map/ppermute | solution.py:23
  48.4 5.9 %collective-permute-done.4 = f32[4,8,16,1]{3,2,1,0:T(8,128)S(1)} collective-permute-done((f32[4,8,16,1]{3,2,1,0:T(8,128)S(1)}, f32[4,8,16,1]{3,2,1,0:T(8,128)S(1)}, u32[]{:S(2)}, u32[]{:S(2)}) %collective-permute-start.4) | collective-permute-done | bytes 2080 | tf_op jit(solution)/shard_map/ppermute | solution.py:22
  54.3 0.3 pad_maximum_fusion.22
  54.6 1.3 collective-permute-start.7
  55.9 3.5 %collective-permute-start.6 = (f32[4,8,1,130]{3,2,1,0:T(1,128)S(1)}, f32[4,8,1,130]{3,2,1,0:T(1,128)S(1)}, u32[]{:S(2)}, u32[]{:S(2)}) collective-permute-start(f32[4,8,1,130]{3,2,1,0:T(1,128)S(1)} %get-tuple-element.17), channel_id=1, source_target_pairs={{0,1},{1,2},{2,3},{4,5},{5,6},{6,7},{8,9},{9,10},{10,11},{12,13},{... | collective-permute-start | bytes 49928 | tf_op jit(solution)/shard_map/ppermute | solution.py:22
  59.5 0.8 collective-permute-done.6
  60.2 0.4 pad_maximum_fusion.11
  60.7 0.6 subtract_multiply_fusion
  61.6 0.3 subtract_multiply_fusion.1
  61.9 0.2 fusion.40
  62.0 0.3 fusion.4
  62.3 1.1 fusion.36
  63.7 73.0 %all-reduce.6.cloned.1.call-done = f32[512,128]{1,0:T(8,128)} async-done(((f32[512,128]{1,0:T(8,128)}), f32[512,128]{1,0:T(8,128)}) %all-reduce.6.cloned.1.call-update) | async-done | bytes 262160 | tf_op jit(solution)/shard_map/psum | solution.py:108
  136.7 1.4 fusion.14
  138.1 0.7 multiply_add_fusion
  (43 shorter events, 1.7 us)
Async XLA Ops:
  6.5 130.2 %all-reduce.6.cloned.1.call-start = ((), (), s32[]{:S(2)}) async-start(), calls=%async_computation | async-start | bytes 524288 | tf_op jit(solution)/shard_map/psum | solution.py:108
  7.4 7.7 %copy-start.3 = (s32[16]{0:T(128)S(1)}, s32[16]{0:T(128)}, u32[]{:S(2)}) copy-start(s32[16]{0:T(128)} %param.9) | copy-start | bytes 196
  7.4 7.8 %copy-start.2 = (s32[8,16,128]{2,1,0:T(8,128)S(1)}, s32[8,16,128]{2,1,0:T(8,128)}, u32[]{:S(2)}) copy-start(s32[8,16,128]{2,1,0:T(8,128)} %param.7) | copy-start | bytes 196612
  7.4 22.0 %copy-start = (f32[4,8,16,128]{3,2,1,0:T(8,128)S(1)}, f32[4,8,16,128]{3,2,1,0:T(8,128)}, u32[]{:S(2)}) copy-start(f32[4,8,16,128]{3,2,1,0:T(8,128)} %param.5) | copy-start | bytes 786436
  7.4 22.0 %copy-start.1 = (f32[8,16,128]{2,1,0:T(8,128)S(1)}, f32[8,16,128]{2,1,0:T(8,128)}, u32[]{:S(2)}) copy-start(f32[8,16,128]{2,1,0:T(8,128)} %param.6) | copy-start | bytes 196612
  8.7 20.6 %collective-permute-start.1 = (f32[6,8,16,1]{3,2,1,0:T(8,128)S(1)}, f32[6,8,16,1]{3,2,1,0:T(8,128)S(1)}, u32[]{:S(2)}, u32[]{:S(2)}) collective-permute-start(f32[6,8,16,1]{3,2,1,0:T(8,128)S(1)} %get-tuple-element.24), channel_id=1, source_target_pairs={{4,0},{8,4},{12,8},{16,12},{20,16},{24,20},{28,24},{0,28},{5,1},{9... | collective-permute-start | bytes 9224 | tf_op jit(solution)/shard_map/ppermute | solution.py:23
  14.7 14.7 %collective-permute-start = (f32[6,8,16,1]{3,2,1,0:T(8,128)S(1)}, f32[6,8,16,1]{3,2,1,0:T(8,128)S(1)}, u32[]{:S(2)}, u32[]{:S(2)}) collective-permute-start(f32[6,8,16,1]{3,2,1,0:T(8,128)S(1)} %get-tuple-element.23), channel_id=1, source_target_pairs={{0,4},{4,8},{8,12},{12,16},{16,20},{20,24},{24,28},{28,0},{1,5},{5... | collective-permute-start | bytes 9224 | tf_op jit(solution)/shard_map/ppermute | solution.py:22
  29.8 3.4 %collective-permute-start.2 = (f32[6,8,1,130]{3,2,1,0:T(1,128)S(1)}, f32[6,8,1,130]{3,2,1,0:T(1,128)S(1)}, u32[]{:S(2)}, u32[]{:S(2)}) collective-permute-start(f32[6,8,1,130]{3,2,1,0:T(1,128)S(1)} %get-tuple-element.10), channel_id=1, source_target_pairs={{0,1},{1,2},{2,3},{4,5},{5,6},{6,7},{8,9},{9,10},{10,11},{12,13},{... | collective-permute-start | bytes 74888 | tf_op jit(solution)/shard_map/ppermute | solution.py:22
  31.7 4.3 %collective-permute-start.3 = (f32[6,8,1,130]{3,2,1,0:T(1,128)S(1)}, f32[6,8,1,130]{3,2,1,0:T(1,128)S(1)}, u32[]{:S(2)}, u32[]{:S(2)}) collective-permute-start(f32[6,8,1,130]{3,2,1,0:T(1,128)S(1)} %get-tuple-element.9), channel_id=1, source_target_pairs={{1,0},{2,1},{3,2},{5,4},{6,5},{7,6},{9,8},{10,9},{11,10},{13,12},{... | collective-permute-start | bytes 74888 | tf_op jit(solution)/shard_map/ppermute | solution.py:23
  38.8 9.6 %collective-permute-start.5 = (f32[4,8,16,1]{3,2,1,0:T(8,128)S(1)}, f32[4,8,16,1]{3,2,1,0:T(8,128)S(1)}, u32[]{:S(2)}, u32[]{:S(2)}) collective-permute-start(f32[4,8,16,1]{3,2,1,0:T(8,128)S(1)} %get-tuple-element.26), channel_id=1, source_target_pairs={{4,0},{8,4},{12,8},{16,12},{20,16},{24,20},{28,24},{0,28},{5,1},{9... | collective-permute-start | bytes 6152 | tf_op jit(solution)/shard_map/ppermute | solution.py:23
  43.6 10.8 %collective-permute-start.4 = (f32[4,8,16,1]{3,2,1,0:T(8,128)S(1)}, f32[4,8,16,1]{3,2,1,0:T(8,128)S(1)}, u32[]{:S(2)}, u32[]{:S(2)}) collective-permute-start(f32[4,8,16,1]{3,2,1,0:T(8,128)S(1)} %get-tuple-element.25), channel_id=1, source_target_pairs={{0,4},{4,8},{8,12},{12,16},{16,20},{20,24},{24,28},{28,0},{1,5},{5... | collective-permute-start | bytes 6152 | tf_op jit(solution)/shard_map/ppermute | solution.py:22
  54.6 4.8 %collective-permute-start.7 = (f32[4,8,1,130]{3,2,1,0:T(1,128)S(1)}, f32[4,8,1,130]{3,2,1,0:T(1,128)S(1)}, u32[]{:S(2)}, u32[]{:S(2)}) collective-permute-start(f32[4,8,1,130]{3,2,1,0:T(1,128)S(1)} %get-tuple-element.18), channel_id=1, source_target_pairs={{1,0},{2,1},{3,2},{5,4},{6,5},{7,6},{9,8},{10,9},{11,10},{13,12},{... | collective-permute-start | bytes 49928 | tf_op jit(solution)/shard_map/ppermute | solution.py:23
  55.9 4.3 %collective-permute-start.6 = (f32[4,8,1,130]{3,2,1,0:T(1,128)S(1)}, f32[4,8,1,130]{3,2,1,0:T(1,128)S(1)}, u32[]{:S(2)}, u32[]{:S(2)}) collective-permute-start(f32[4,8,1,130]{3,2,1,0:T(1,128)S(1)} %get-tuple-element.17), channel_id=1, source_target_pairs={{0,1},{1,2},{2,3},{4,5},{5,6},{6,7},{8,9},{9,10},{10,11},{12,13},{... | collective-permute-start | bytes 49928 | tf_op jit(solution)/shard_map/ppermute | solution.py:22
  62.0 1.5 copy-start.4
Sparse Core Ops, SparseCore 0:
  63.6 73.0 all-reduce.5
where the time goes:
time: 146 us
  waiting for transfers between devices  101 us (69%)
  starting transfers between devices  18.9 us (13%)
  between operations  13.7 us (9%)
  other arithmetic  7.99 us (5%)
  matrix products  2.53 us (2%)
    psum x1, waiting for transfers between devices, shards(): totals = lax.psum(partial_sum, 'lon')  73 us
    ppermute x4, waiting for transfers between devices, with_halo(): after = lax.ppermute(leading, axis, down)  21.6 us
    ppermute x4, starting transfers between devices, with_halo(): after = lax.ppermute(leading, axis, down)  13.5 us
    ppermute x4, waiting for transfers between devices, with_halo(): before = lax.ppermute(last, axis, up)  6.89 us
    ppermute x4, starting transfers between devices, with_halo(): before = lax.ppermute(last, axis, up)  5.41 us
  transfers between devices with their start and end apart: 9, of which 7 were waited for; matrix products, arithmetic and copies ran while one was open for 1% of the time, Pallas kernels for 0%

commit v1 on v0

--- a/solution.py
+++ b/solution.py
@@ -105,7 +105,7 @@
     partial_sum = jnp.dot(
         flat, basis, precision=lax.Precision.HIGHEST, preferred_element_type=jnp.float32
     )
-    totals = lax.psum(partial_sum, "lon")
+    totals = jnp.sum(lax.all_gather(partial_sum, "lon"), axis=0)
     smooth = jnp.dot(
         totals * mode_weights(row_counts, MAXM, nlon),
         basis.T,

time: 146 us -> 125 us (0.86)
  waiting for transfers between devices: 101 us -> 80.2 us
  other arithmetic: 7.99 us -> 9.71 us
    psum x1 -> x0, waiting for transfers between devices: 73 us -> none  [shards(): totals = lax.psum(partial_sum, 'lon')]
    all_gather x0 -> x1, waiting for transfers between devices: none -> 51.6 us  [shards(): totals = jnp.sum(lax.all_gather(partial_sum, 'lon'), axis=0)]
    reduce_sum x0 -> x1, other arithmetic: none -> 1.72 us  [shards(): totals = jnp.sum(lax.all_gather(partial_sum, 'lon'), axis=0)]
where the time goes in v1:
time: 125 us
  waiting for transfers between devices  80.2 us (64%)
  starting transfers between devices  18.9 us (15%)
  between operations  13.7 us (11%)
  other arithmetic  9.71 us (8%)
  matrix products  1.6 us (1%)
    all_gather x1, waiting for transfers between devices, shards(): totals = jnp.sum(lax.all_gather(partial_sum, 'lon'), axis=0)  51.6 us
    ppermute x4, waiting for transfers between devices, with_halo(): after = lax.ppermute(leading, axis, down)  21.7 us
    ppermute x4, starting transfers between devices, with_halo(): after = lax.ppermute(leading, axis, down)  13.5 us
    ppermute x4, waiting for transfers between devices, with_halo(): before = lax.ppermute(last, axis, up)  6.89 us
    ppermute x4, starting transfers between devices, with_halo(): before = lax.ppermute(last, axis, up)  5.41 us
  transfers between devices with their start and end apart: 9, of which 7 were waited for; matrix products, arithmetic and copies ran while one was open for 1% of the time, Pallas kernels for 0%

profile of v1, /device:TPU:0, one launch (start us, length us, event | category | flops | bytes accessed | tf_op | source)
XLA Modules:
  0.0 125.2 jit_solution(9615597959738636014)
XLA Ops:
  6.5 0.8 convert_bitcast_fusion
  7.4 1.1 pad_maximum_fusion.13
  8.4 0.2 fusion.44
  8.6 6.1 %collective-permute-start.1 = (f32[6,8,16,1]{3,2,1,0:T(8,128)S(1)}, f32[6,8,16,1]{3,2,1,0:T(8,128)S(1)}, u32[]{:S(2)}, u32[]{:S(2)}) collective-permute-start(f32[6,8,16,1]{3,2,1,0:T(8,128)S(1)} %get-tuple-element.24), channel_id=1, source_target_pairs={{4,0},{8,4},{12,8},{16,12},{20,16},{24,20},{28,24},{0,28},{5,1},{9... | collective-permute-start | bytes 9224 | tf_op jit(solution)/shard_map/ppermute | solution.py:23
  14.9 14.3 %collective-permute-done.1 = f32[6,8,16,1]{3,2,1,0:T(8,128)S(1)} collective-permute-done((f32[6,8,16,1]{3,2,1,0:T(8,128)S(1)}, f32[6,8,16,1]{3,2,1,0:T(8,128)S(1)}, u32[]{:S(2)}, u32[]{:S(2)}) %collective-permute-start.1) | collective-permute-done | bytes 3104 | tf_op jit(solution)/shard_map/ppermute | solution.py:23
  29.4 0.4 pad_maximum_fusion.15
  29.7 1.9 %collective-permute-start.2 = (f32[6,8,1,130]{3,2,1,0:T(1,128)S(1)}, f32[6,8,1,130]{3,2,1,0:T(1,128)S(1)}, u32[]{:S(2)}, u32[]{:S(2)}) collective-permute-start(f32[6,8,1,130]{3,2,1,0:T(1,128)S(1)} %get-tuple-element.10), channel_id=1, source_target_pairs={{0,1},{1,2},{2,3},{4,5},{5,6},{6,7},{8,9},{9,10},{10,11},{12,13},{... | collective-permute-start | bytes 74888 | tf_op jit(solution)/shard_map/ppermute | solution.py:22
  31.7 1.3 %collective-permute-start.3 = (f32[6,8,1,130]{3,2,1,0:T(1,128)S(1)}, f32[6,8,1,130]{3,2,1,0:T(1,128)S(1)}, u32[]{:S(2)}, u32[]{:S(2)}) collective-permute-start(f32[6,8,1,130]{3,2,1,0:T(1,128)S(1)} %get-tuple-element.9), channel_id=1, source_target_pairs={{1,0},{2,1},{3,2},{5,4},{6,5},{7,6},{9,8},{10,9},{11,10},{13,12},{... | collective-permute-start | bytes 74888 | tf_op jit(solution)/shard_map/ppermute | solution.py:23
  33.1 2.9 %collective-permute-done.3 = f32[6,8,1,130]{3,2,1,0:T(1,128)S(1)} collective-permute-done((f32[6,8,1,130]{3,2,1,0:T(1,128)S(1)}, f32[6,8,1,130]{3,2,1,0:T(1,128)S(1)}, u32[]{:S(2)}, u32[]{:S(2)}) %collective-permute-start.3) | collective-permute-done | bytes 24992 | tf_op jit(solution)/shard_map/ppermute | solution.py:23
  36.0 0.5 pad_maximum_fusion
  36.8 0.6 subtract_multiply_fusion.2
  37.5 0.2 fusion.23
  37.7 0.3 subtract_multiply_fusion.3
  38.3 0.3 fusion.11
  38.7 4.8 %collective-permute-start.5 = (f32[4,8,16,1]{3,2,1,0:T(8,128)S(1)}, f32[4,8,16,1]{3,2,1,0:T(8,128)S(1)}, u32[]{:S(2)}, u32[]{:S(2)}) collective-permute-start(f32[4,8,16,1]{3,2,1,0:T(8,128)S(1)} %get-tuple-element.26), channel_id=1, source_target_pairs={{4,0},{8,4},{12,8},{16,12},{20,16},{24,20},{28,24},{0,28},{5,1},{9... | collective-permute-start | bytes 6152 | tf_op jit(solution)/shard_map/ppermute | solution.py:23
  43.6 0.3 fusion.35
  43.9 4.5 %collective-permute-done.5 = f32[4,8,16,1]{3,2,1,0:T(8,128)S(1)} collective-permute-done((f32[4,8,16,1]{3,2,1,0:T(8,128)S(1)}, f32[4,8,16,1]{3,2,1,0:T(8,128)S(1)}, u32[]{:S(2)}, u32[]{:S(2)}) %collective-permute-start.5) | collective-permute-done | bytes 2080 | tf_op jit(solution)/shard_map/ppermute | solution.py:23
  48.4 5.9 %collective-permute-done.4 = f32[4,8,16,1]{3,2,1,0:T(8,128)S(1)} collective-permute-done((f32[4,8,16,1]{3,2,1,0:T(8,128)S(1)}, f32[4,8,16,1]{3,2,1,0:T(8,128)S(1)}, u32[]{:S(2)}, u32[]{:S(2)}) %collective-permute-start.4) | collective-permute-done | bytes 2080 | tf_op jit(solution)/shard_map/ppermute | solution.py:22
  54.3 0.3 pad_maximum_fusion.22
  54.6 1.3 %collective-permute-start.7 = (f32[4,8,1,130]{3,2,1,0:T(1,128)S(1)}, f32[4,8,1,130]{3,2,1,0:T(1,128)S(1)}, u32[]{:S(2)}, u32[]{:S(2)}) collective-permute-start(f32[4,8,1,130]{3,2,1,0:T(1,128)S(1)} %get-tuple-element.18), channel_id=1, source_target_pairs={{1,0},{2,1},{3,2},{5,4},{6,5},{7,6},{9,8},{10,9},{11,10},{13,12},{... | collective-permute-start | bytes 49928 | tf_op jit(solution)/shard_map/ppermute | solution.py:23
  55.9 3.5 %collective-permute-start.6 = (f32[4,8,1,130]{3,2,1,0:T(1,128)S(1)}, f32[4,8,1,130]{3,2,1,0:T(1,128)S(1)}, u32[]{:S(2)}, u32[]{:S(2)}) collective-permute-start(f32[4,8,1,130]{3,2,1,0:T(1,128)S(1)} %get-tuple-element.17), channel_id=1, source_target_pairs={{0,1},{1,2},{2,3},{4,5},{5,6},{6,7},{8,9},{9,10},{10,11},{12,13},{... | collective-permute-start | bytes 49928 | tf_op jit(solution)/shard_map/ppermute | solution.py:22
  59.4 0.8 collective-permute-done.6
  60.2 0.4 pad_maximum_fusion.11
  60.7 0.6 subtract_multiply_fusion
  61.5 0.3 subtract_multiply_fusion.1
  61.8 0.2 fusion.40
  62.0 0.3 fusion.4
  62.3 1.1 fusion.36
  63.8 51.6 %all-gather.3.cloned.1.call-done = f32[4096,128]{1,0:T(8,128)} async-done(((f32[512,128]{1,0:T(8,128)}), f32[4096,128]{1,0:T(8,128)}) %all-gather.3.cloned.1.call-update) | async-done | bytes 2097168 | tf_op jit(solution)/shard_map/all_gather | solution.py:108
  115.4 1.7 %reduce_sum.9 = f32[512,128]{1,0:T(8,128)S(1)} reduce(f32[8,512,128]{2,1,0:T(8,128)} %bitcast.20, f32[]{:T(128)} %constant.27.clone.1), dimensions={0}, to_apply=%region_0.1 | reduce | flops 458752 | bytes 2359300 | tf_op jit(solution)/shard_map/reduce_sum | solution.py:108
  117.1 0.5 fusion.14
  117.6 0.7 multiply_add_fusion
  (44 shorter events, 1.8 us)
Async XLA Ops:
  6.5 108.9 %all-gather.3.cloned.1.call-start = ((), (), s32[]{:S(2)}) async-start(), calls=%async_computation | async-start | bytes 2359296 | tf_op jit(solution)/shard_map/all_gather | solution.py:108
  7.4 22.0 %copy-start = (f32[4,8,16,128]{3,2,1,0:T(8,128)S(1)}, f32[4,8,16,128]{3,2,1,0:T(8,128)}, u32[]{:S(2)}) copy-start(f32[4,8,16,128]{3,2,1,0:T(8,128)} %param.5) | copy-start | bytes 786436
  7.4 22.0 %copy-start.1 = (f32[8,16,128]{2,1,0:T(8,128)S(1)}, f32[8,16,128]{2,1,0:T(8,128)}, u32[]{:S(2)}) copy-start(f32[8,16,128]{2,1,0:T(8,128)} %param.6) | copy-start | bytes 196612
  8.6 20.6 %collective-permute-start.1 = (f32[6,8,16,1]{3,2,1,0:T(8,128)S(1)}, f32[6,8,16,1]{3,2,1,0:T(8,128)S(1)}, u32[]{:S(2)}, u32[]{:S(2)}) collective-permute-start(f32[6,8,16,1]{3,2,1,0:T(8,128)S(1)} %get-tuple-element.24), channel_id=1, source_target_pairs={{4,0},{8,4},{12,8},{16,12},{20,16},{24,20},{28,24},{0,28},{5,1},{9... | collective-permute-start | bytes 9224 | tf_op jit(solution)/shard_map/ppermute | solution.py:23
  14.7 14.7 %collective-permute-start = (f32[6,8,16,1]{3,2,1,0:T(8,128)S(1)}, f32[6,8,16,1]{3,2,1,0:T(8,128)S(1)}, u32[]{:S(2)}, u32[]{:S(2)}) collective-permute-start(f32[6,8,16,1]{3,2,1,0:T(8,128)S(1)} %get-tuple-element.23), channel_id=1, source_target_pairs={{0,4},{4,8},{8,12},{12,16},{16,20},{20,24},{24,28},{28,0},{1,5},{5... | collective-permute-start | bytes 9224 | tf_op jit(solution)/shard_map/ppermute | solution.py:22
  29.7 3.3 %collective-permute-start.2 = (f32[6,8,1,130]{3,2,1,0:T(1,128)S(1)}, f32[6,8,1,130]{3,2,1,0:T(1,128)S(1)}, u32[]{:S(2)}, u32[]{:S(2)}) collective-permute-start(f32[6,8,1,130]{3,2,1,0:T(1,128)S(1)} %get-tuple-element.10), channel_id=1, source_target_pairs={{0,1},{1,2},{2,3},{4,5},{5,6},{6,7},{8,9},{9,10},{10,11},{12,13},{... | collective-permute-start | bytes 74888 | tf_op jit(solution)/shard_map/ppermute | solution.py:22
  31.7 4.3 %collective-permute-start.3 = (f32[6,8,1,130]{3,2,1,0:T(1,128)S(1)}, f32[6,8,1,130]{3,2,1,0:T(1,128)S(1)}, u32[]{:S(2)}, u32[]{:S(2)}) collective-permute-start(f32[6,8,1,130]{3,2,1,0:T(1,128)S(1)} %get-tuple-element.9), channel_id=1, source_target_pairs={{1,0},{2,1},{3,2},{5,4},{6,5},{7,6},{9,8},{10,9},{11,10},{13,12},{... | collective-permute-start | bytes 74888 | tf_op jit(solution)/shard_map/ppermute | solution.py:23
  38.7 9.6 %collective-permute-start.5 = (f32[4,8,16,1]{3,2,1,0:T(8,128)S(1)}, f32[4,8,16,1]{3,2,1,0:T(8,128)S(1)}, u32[]{:S(2)}, u32[]{:S(2)}) collective-permute-start(f32[4,8,16,1]{3,2,1,0:T(8,128)S(1)} %get-tuple-element.26), channel_id=1, source_target_pairs={{4,0},{8,4},{12,8},{16,12},{20,16},{24,20},{28,24},{0,28},{5,1},{9... | collective-permute-start | bytes 6152 | tf_op jit(solution)/shard_map/ppermute | solution.py:23
  43.6 10.8 %collective-permute-start.4 = (f32[4,8,16,1]{3,2,1,0:T(8,128)S(1)}, f32[4,8,16,1]{3,2,1,0:T(8,128)S(1)}, u32[]{:S(2)}, u32[]{:S(2)}) collective-permute-start(f32[4,8,16,1]{3,2,1,0:T(8,128)S(1)} %get-tuple-element.25), channel_id=1, source_target_pairs={{0,4},{4,8},{8,12},{12,16},{16,20},{20,24},{24,28},{28,0},{1,5},{5... | collective-permute-start | bytes 6152 | tf_op jit(solution)/shard_map/ppermute | solution.py:22
  54.6 4.8 %collective-permute-start.7 = (f32[4,8,1,130]{3,2,1,0:T(1,128)S(1)}, f32[4,8,1,130]{3,2,1,0:T(1,128)S(1)}, u32[]{:S(2)}, u32[]{:S(2)}) collective-permute-start(f32[4,8,1,130]{3,2,1,0:T(1,128)S(1)} %get-tuple-element.18), channel_id=1, source_target_pairs={{1,0},{2,1},{3,2},{5,4},{6,5},{7,6},{9,8},{10,9},{11,10},{13,12},{... | collective-permute-start | bytes 49928 | tf_op jit(solution)/shard_map/ppermute | solution.py:23
  55.9 4.3 %collective-permute-start.6 = (f32[4,8,1,130]{3,2,1,0:T(1,128)S(1)}, f32[4,8,1,130]{3,2,1,0:T(1,128)S(1)}, u32[]{:S(2)}, u32[]{:S(2)}) collective-permute-start(f32[4,8,1,130]{3,2,1,0:T(1,128)S(1)} %get-tuple-element.17), channel_id=1, source_target_pairs={{0,1},{1,2},{2,3},{4,5},{5,6},{6,7},{8,9},{9,10},{10,11},{12,13},{... | collective-permute-start | bytes 49928 | tf_op jit(solution)/shard_map/ppermute | solution.py:22
  62.0 1.5 %copy-start.3 = (s32[16]{0:T(128)S(1)}, s32[16]{0:T(128)}, u32[]{:S(2)}) copy-start(s32[16]{0:T(128)} %param.8) | copy-start | bytes 196
  62.0 1.6 %copy-start.4 = (s32[16]{0:T(128)S(1)}, s32[16]{0:T(128)}, u32[]{:S(2)}) copy-start(s32[16]{0:T(128)} %param.9) | copy-start | bytes 196
  62.0 1.6 %copy-start.2 = (s32[8,16,128]{2,1,0:T(8,128)S(1)}, s32[8,16,128]{2,1,0:T(8,128)}, u32[]{:S(2)}) copy-start(s32[8,16,128]{2,1,0:T(8,128)} %param.7) | copy-start | bytes 196612
Sparse Core Ops, SparseCore 0:
  63.6 51.7 all-gather.2
